TPU v7x, 32 devices: a whole 2x2x4 slice. The times are simulated.
32 devices in a mesh: row: 4 (over x, core), col: 8 (over z, y).
Axes of the slice: x: 2, y: 2, z: 4, core: 2. Of those that a mesh axis runs over, the one named last changes fastest.
Arguments:
- pair: bfloat16 [768, 768, 512], P('row', 'col'), may hold values from -6 to 6
- w_bias: bfloat16 [512, 96], replicated, may hold values from -0.25 to 0.25
- queries: bfloat16 [768, 1536], P('row', 'col'), may hold values from -360 to 360
- keys: bfloat16 [768, 1536], P('col', 'row'), may hold values from -6 to 6
- values: bfloat16 [768, 1536], P('col', 'row'), may hold values from -6 to 6
- d_out: bfloat16 [768, 1536], P('row', 'col'), may hold values from -6 to 6
Outputs:
- d_pair: bfloat16 [768, 768, 512], P('row', 'col')
- d_wbias: float32 [512, 96], replicated
- d_queries: bfloat16 [768, 1536], P('row', 'col')
- d_keys: bfloat16 [768, 1536], P('col', 'row')
- d_values: bfloat16 [768, 1536], P('col', 'row')
All inputs are finite; a program needn't handle non-finite values.
Results may differ from a plain program's by a relative error of at most 0.0095.
Values may be sent and summed in bfloat16 or wider, within the bound.
A program may use at most 128 MiB of HBM per device.

v0:
```python
import jax
import jax.numpy as jnp
from jax import lax
from jax.sharding import PartitionSpec as P

D = 1536
H = 96
P_SIZE = 512
HD = 16


def joined(value, axis, join):
    pieces = jax.tree.map(lambda part: lax.all_gather(part, axis), value)
    head = jax.tree.map(lambda part: part[0], pieces)
    tail = jax.tree.map(lambda part: part[1:], pieces)
    subtotal, _ = lax.scan(lambda subtotal, piece: (join(subtotal, piece), None), head, tail)
    return subtotal


def combine_stats(former, latter):
    joined_max = jnp.maximum(former[0], latter[0])
    scale_former = jnp.exp(former[0] - joined_max)
    scale_latter = jnp.exp(latter[0] - joined_max)
    return (
        joined_max,
        former[1] * scale_former + latter[1] * scale_latter,
        former[2] * scale_former + latter[2] * scale_latter,
    )


def on_device(pair, w_bias, queries, keys, values, d_out):
    row_count = pair.shape[0]
    col_count = pair.shape[1]
    query_full, out_full = (
        lax.all_gather(queries, "col", axis=1, tiled=True),
        lax.all_gather(d_out, "col", axis=1, tiled=True),
    )
    key_full, value_full = (
        lax.all_gather(keys, "row", axis=1, tiled=True),
        lax.all_gather(values, "row", axis=1, tiled=True),
    )
    query_heads = query_full.reshape(row_count, H, HD)
    out_heads = out_full.reshape(row_count, H, HD)
    key_heads = key_full.reshape(col_count, H, HD)
    value_heads = value_full.reshape(col_count, H, HD)
    flat_pair = pair.reshape(row_count * col_count, P_SIZE)
    pair_bias = jnp.dot(flat_pair, w_bias, preferred_element_type=jnp.float32).reshape(
        row_count, col_count, H
    )
    scale = 1.0 / HD**0.5
    scores = jnp.einsum(
        "ihd,jhd->hij", query_heads, key_heads, preferred_element_type=jnp.float32
    ) * scale + pair_bias.transpose(2, 0, 1)
    grad_prob = jnp.einsum(
        "ihd,jhd->hij", out_heads, value_heads, preferred_element_type=jnp.float32
    )
    local_max = jnp.max(scores, axis=-1)
    exp_scores = jnp.exp(scores - local_max[..., None])
    local_stats = (
        local_max,
        jnp.sum(exp_scores, axis=-1),
        jnp.sum(exp_scores * grad_prob, axis=-1),
    )
    row_max, row_total, row_upper = joined(local_stats, "col", combine_stats)
    weights = jnp.exp(scores - row_max[..., None]) / row_total[..., None]
    row_delta = row_upper / row_total
    grad_score = (weights * (grad_prob - row_delta[..., None])).astype(jnp.bfloat16)
    weights_low = weights.astype(jnp.bfloat16)
    score_flat = grad_score.transpose(1, 2, 0).reshape(row_count * col_count, H)
    d_pair = (
        jnp.dot(score_flat, w_bias.T, preferred_element_type=jnp.float32)
        .astype(jnp.bfloat16)
        .reshape(row_count, col_count, P_SIZE)
    )
    weight_term = jnp.dot(flat_pair.T, score_flat, preferred_element_type=jnp.float32)
    d_wbias = lax.psum(weight_term, ("row", "col"))
    query_term = (
        jnp.einsum("hij,jhd->ihd", grad_score, key_heads, preferred_element_type=jnp.float32)
        * scale
    ).reshape(row_count, D)
    key_term = (
        jnp.einsum("hij,ihd->jhd", grad_score, query_heads, preferred_element_type=jnp.float32)
        * scale
    ).reshape(col_count, D)
    value_term = jnp.einsum(
        "hij,ihd->jhd", weights_low, out_heads, preferred_element_type=jnp.float32
    ).reshape(col_count, D)
    query_grad = lax.psum_scatter(query_term, "col", scatter_dimension=1, tiled=True)
    key_grad, value_grad = (
        lax.psum_scatter(key_term, "row", scatter_dimension=1, tiled=True),
        lax.psum_scatter(value_term, "row", scatter_dimension=1, tiled=True),
    )
    return (
        d_pair,
        d_wbias,
        query_grad.astype(jnp.bfloat16),
        key_grad.astype(jnp.bfloat16),
        value_grad.astype(jnp.bfloat16),
    )


def solution(mesh):
    return jax.shard_map(
        on_device,
        mesh=mesh,
        in_specs=(
            P("row", "col", None),
            P(),
            P("row", "col"),
            P("col", "row"),
            P("col", "row"),
            P("row", "col"),
        ),
        out_specs=(P("row", "col", None), P(), P("row", "col"), P("col", "row"), P("col", "row")),
        check_vma=False,
    )
```

profile of v0, /device:TPU:8, one launch (start us, length us, event | category | flops | bytes accessed | tf_op | source)
XLA Modules:
  0.0 433.7 jit_solution(17199849973470065205)
XLA Ops:
  8.9 11.2 %fusion.11 = f32[192,96,96]{2,1,0:T(8,128)} fusion(bf16[192,96,512]{2,1,0:T(8,128)(2,1)} %param.8, bf16[512,96]{0,1:T(8,128)(2,1)S(1)} %copy-done), kind=kOutput, calls=%fused_computation.27 | convolution fusion | flops 1811939328 | bytes 26050560 | tf_op jit(solution)/shard_map/dot_general | solution.py:47
  20.1 12.1 %copy.40 = f32[192,96,96]{0,1,2:T(8,128)} copy(f32[192,96,96]{2,1,0:T(8,128)} %fusion.11) | data formatting | bytes 14155776 | tf_op jit(solution)/shard_map/dot_general | solution.py:47
  32.4 29.7 %all_gather.30 = bf16[192,1536]{0,1:T(8,128)(2,1)S(1)} all-gather(bf16[192,192]{0,1:T(8,128)(2,1)S(1)} %copy.38), channel_id=1, replica_groups=mesh['row'=4,'col'=8] {'col'}, dimensions={1}, use_global_device_ids=true | all-gather | bytes 663552 | tf_op jit(solution)/shard_map/all_gather | solution.py:35
  62.1 5.9 %all_gather.31 = bf16[96,1536]{1,0:T(8,128)(2,1)S(1)} all-gather(bf16[96,384]{1,0:T(8,128)(2,1)S(1)} %copy-done.5), channel_id=1, replica_groups=mesh['row'=4,'col'=8] {'row'}, dimensions={1}, use_global_device_ids=true | all-gather | bytes 368640 | tf_op jit(solution)/shard_map/all_gather | solution.py:39
  68.4 32.2 %all_gather.36 = bf16[192,1536]{0,1:T(8,128)(2,1)S(1)} all-gather(bf16[192,192]{0,1:T(8,128)(2,1)S(1)} %copy.42), channel_id=1, replica_groups=mesh['row'=4,'col'=8] {'col'}, dimensions={1}, use_global_device_ids=true | all-gather | bytes 663552 | tf_op jit(solution)/shard_map/all_gather | solution.py:36
  100.6 5.9 %all_gather.37 = bf16[96,1536]{1,0:T(8,128)(2,1)S(1)} all-gather(bf16[96,384]{1,0:T(8,128)(2,1)S(1)} %copy-done.6), channel_id=1, replica_groups=mesh['row'=4,'col'=8] {'row'}, dimensions={1}, use_global_device_ids=true | all-gather | bytes 368640 | tf_op jit(solution)/shard_map/all_gather | solution.py:40
  106.7 9.2 %fusion.13 = (f32[96,192]{1,0:T(8,128)S(1)}, f32[96,192,96]{1,2,0:T(8,128)S(1)}, f32[96,192,96]{1,2,0:T(8,128)}) fusion(f32[192,96,96]{0,1,2:T(8,128)} %copy.40, bf16[192,96,16]{0,2,1:T(8,128)(2,1)S(1)} %bitcast.92, bf16[96,96,16]{0,2,1:T(8,128)(2,1)S(1)} %bitcast.96), kind=kOutput, calls=%fused_computation.29 | convolution fusion | flops 61913088 | bytes 22192128 | tf_op jit(solution)/shard_map/ihd,jhd->hij/dot_general | solution.py:51
  115.8 5.7 %multiply_reduce_fusion = (f32[96,192]{1,0:T(8,128)S(1)}, f32[96,192]{1,0:T(8,128)S(1)}, f32[96,192,96]{1,2,0:T(8,128)}) fusion(f32[96,192,96]{1,2,0:T(8,128)S(1)} %get-tuple-element.66, f32[96,192]{1,0:T(8,128)S(1)} %get-tuple-element.65, bf16[192,96,16]{0,2,1:T(8,128)(2,1)S(1)} %bitcast.98, bf16[96,96,16]{0,2,1:T(8,128)(2,1)S(1)} %bitcast.103), kind=kOutput, calls=%fused_computation.19 | convolution fusion | flops 63664128 | bytes 15261696 | tf_op jit(solution)/shard_map/ihd,jhd->hij/dot_general | solution.py:54
  122.1 32.1 %all-gather.1 = f32[768,192]{1,0:T(8,128)S(1)} all-gather(f32[96,192]{1,0:T(8,128)S(1)} %get-tuple-element.48), channel_id=3, replica_groups=mesh['row'=4,'col'=8] {'col'}, dimensions={0}, use_global_device_ids=true | all-gather | bytes 663552 | tf_op jit(solution)/shard_map/all_gather | solution.py:13
  155.2 32.1 %all-gather.2 = f32[768,192]{1,0:T(8,128)S(1)} all-gather(f32[96,192]{1,0:T(8,128)S(1)} %get-tuple-element.47), channel_id=4, replica_groups=mesh['row'=4,'col'=8] {'col'}, dimensions={0}, use_global_device_ids=true | all-gather | bytes 663552 | tf_op jit(solution)/shard_map/all_gather | solution.py:13
  188.2 32.0 %all-gather = f32[768,192]{1,0:T(8,128)S(1)} all-gather(f32[96,192]{1,0:T(8,128)S(1)} %get-tuple-element.65), channel_id=2, replica_groups=mesh['row'=4,'col'=8] {'col'}, dimensions={0}, use_global_device_ids=true | all-gather | bytes 663552 | tf_op jit(solution)/shard_map/all_gather | solution.py:13
  220.3 13.8 %while.14 = (s32[]{:T(128)}, f32[96,192]{1,0:T(8,128)S(1)}, f32[96,192]{1,0:T(8,128)S(1)}, f32[96,192]{1,0:T(8,128)S(1)}, f32[7,96,192]{2,1,0:T(8,128)S(1)}, /*i...) while((s32[]{:T(128)}, f32[96,192]{1,0:T(8,128)S(1)}, f32[96,192]{1,0:T(8,128)S(1)}, ...), condition=%wide.region_4.5_spmd, body=%wide.region_3.4_spmd.sunk | while | flops 202754 | bytes 1032285 | solution.py:16
  234.2 6.2 %fusion.9 = f32[96,96,16]{1,2,0:T(8,128)} fusion(bf16[192,96,16]{0,2,1:T(8,128)(2,1)S(1)} %bitcast.99, f32[96,192,96]{1,2,0:T(8,128)} %copy-done.1, f32[96,192]{1,0:T(8,128)S(1)} %get-tuple-element.45, f32[96,192]{1,0:T(8,128)S(1)} %get-tuple-element.44), kind=kOutput, calls=%fused_computation.22 | convolution fusion | flops 61931520 | bytes 8404992 | tf_op jit(solution)/shard_map/hij,ihd->jhd/dot_general | solution.py:85
  240.3 2.2 copy.51
  242.8 7.9 %multiply_convert_fusion = bf16[96,192,96]{1,2,0:T(8,128)(2,1)S(1)} fusion(f32[96,192,96]{1,2,0:T(8,128)} %get-tuple-element.68, f32[96,192]{1,0:T(8,128)S(1)} %div.21, f32[96,192]{1,0:T(8,128)S(1)} %get-tuple-element.45, f32[96,192,96]{1,2,0:T(8,128)} %copy-done.1, f32[96,192]{1,0:T(8,128)S(1)} %get-tuple-element.44), kind=kLoop, calls=%fused_computation.17 | loop fusion | flops 8847360 | bytes 17915904 | tf_op jit(solution)/shard_map/convert_element_type | solution.py:67
  255.4 4.2 convolution_multiply_fusion
  259.7 13.1 %fusion.4 = bf16[192,96,96]{0,1,2:T(8,128)(2,1)} fusion(f32[96,192,96]{1,2,0:T(8,128)} %get-tuple-element.68, f32[192,96,96]{0,1,2:T(8,128)} %copy.40, f32[96,192,96]{1,2,0:T(8,128)} %get-tuple-element.67, f32[192,96]{0,1:T(8,128)S(1)} %bitcast.104, f32[192,96]{0,1:T(8,128)S(1)} %bitcast.91, f32[192,96]{0,1:T(8,128)S(1)} %bitcast.90), kind=kLoop, calls=%fused_computation.11 | loop fusion | flops 12386304 | bytes 24993792 | tf_op jit(solution)/shard_map/convert_element_type | solution.py:67
  272.8 7.6 %copy.45 = bf16[192,96,96]{1,2,0:T(8,128)(2,1)} copy(bf16[192,96,96]{0,1,2:T(8,128)(2,1)} %fusion.4) | data formatting | bytes 7077888 | tf_op jit(solution)/shard_map/convert_element_type | solution.py:67
  280.5 11.8 %convolution_bitcast_fusion = f32[512,96]{0,1:T(8,128)} fusion(bf16[192,96,96]{1,2,0:T(8,128)(2,1)} %copy.45, bf16[192,96,512]{2,1,0:T(8,128)(2,1)} %param.8), kind=kOutput, calls=%fused_computation.26 | convolution fusion | flops 1811939328 | bytes 22609920 | tf_op jit(solution)/shard_map/dot_general | solution.py:75
  292.2 6.7 %copy.44 = bf16[192,96,96]{1,0,2:T(8,128)(2,1)} copy(bf16[192,96,96]{0,1,2:T(8,128)(2,1)} %fusion.4) | data formatting | bytes 7077888 | tf_op jit(solution)/shard_map/convert_element_type | solution.py:67
  299.0 9.2 %reshape.49 = bf16[18432,96]{0,1:T(8,128)(2,1)} reshape(bf16[192,96,96]{1,0,2:T(8,128)(2,1)} %copy.44) | data formatting | bytes 7077888 | tf_op jit(solution)/shard_map/reshape | solution.py:69
  308.2 11.5 %convolution_convert_fusion = bf16[18432,512]{1,0:T(8,128)(2,1)} fusion(bf16[18432,96]{0,1:T(8,128)(2,1)} %reshape.49, bf16[512,96]{0,1:T(8,128)(2,1)S(1)} %copy-done), kind=kOutput, calls=%fused_computation.8 | convolution fusion | flops 1821376512 | bytes 22511616 | tf_op jit(solution)/shard_map/dot_general | solution.py:71
  322.8 38.5 %reduce-scatter.10.cloned.1.call-done = f32[192,192]{1,0:T(8,128)} async-done(((f32[1536,192]{1,0:T(8,128)}), f32[192,192]{1,0:T(8,128)}) %reduce-scatter.10.cloned.1.call-update) | async-done | bytes 147472
  363.0 61.9 %all-reduce.2.cloned.1.call-done = f32[512,96]{0,1:T(8,128)} async-done(((f32[512,96]{0,1:T(8,128)}), f32[512,96]{0,1:T(8,128)}) %all-reduce.2.cloned.1.call-update) | async-done | bytes 196624 | tf_op jit(solution)/shard_map/psum | solution.py:76
  (62 shorter events, 29.1 us)
Async XLA Ops:
  8.0 0.9 copy-start
  8.0 311.7 %reduce-scatter.8.cloned.1.call-start = ((), (), s32[]{:S(2)}) async-start(), calls=%async_computation.5 | async-start | bytes 737280 | tf_op jit(solution)/shard_map/reduce_scatter | solution.py:91
  20.1 12.2 %copy-start.3 = (bf16[192,192]{1,0:T(8,128)(2,1)S(1)}, bf16[192,192]{1,0:T(8,128)(2,1)}, u32[]{:S(2)}) copy-start(bf16[192,192]{1,0:T(8,128)(2,1)} %param.10) | copy-start | bytes 221188
  20.1 42.0 %copy-start.5 = (bf16[96,384]{1,0:T(8,128)(2,1)S(1)}, bf16[96,384]{1,0:T(8,128)(2,1)}, u32[]{:S(2)}) copy-start(bf16[96,384]{1,0:T(8,128)(2,1)} %param.11) | copy-start | bytes 221188
  20.1 48.1 %copy-start.4 = (bf16[192,192]{1,0:T(8,128)(2,1)S(1)}, bf16[192,192]{1,0:T(8,128)(2,1)}, u32[]{:S(2)}) copy-start(bf16[192,192]{1,0:T(8,128)(2,1)} %param.13) | copy-start | bytes 221188
  20.1 80.5 %copy-start.6 = (bf16[96,384]{1,0:T(8,128)(2,1)S(1)}, bf16[96,384]{1,0:T(8,128)(2,1)}, u32[]{:S(2)}) copy-start(bf16[96,384]{1,0:T(8,128)(2,1)} %param.12) | copy-start | bytes 221188
  115.8 6.3 %copy-start.1 = (f32[96,192,96]{1,2,0:T(8,128)}, f32[96,192,96]{1,2,0:T(8,128)S(1)}, u32[]{:S(2)}) copy-start(f32[96,192,96]{1,2,0:T(8,128)S(1)} %get-tuple-element.66) | copy-start | bytes 21233668
  242.6 78.7 %reduce-scatter.6.cloned.1.call-start = ((), (), s32[]{:S(2)}) async-start(), calls=%async_computation.4 | async-start | bytes 737280 | tf_op jit(solution)/shard_map/reduce_scatter | solution.py:90
  250.7 2.2 copy-start.2
  255.4 106.0 %reduce-scatter.10.cloned.1.call-start = ((), (), s32[]{:S(2)}) async-start(), calls=%async_computation.6 | async-start | bytes 1769472
  259.7 165.3 %all-reduce.2.cloned.1.call-start = ((), (), s32[]{:S(2)}) async-start(), calls=%async_computation.3 | async-start | bytes 393216 | tf_op jit(solution)/shard_map/psum | solution.py:76
Sparse Core Ops, SparseCore 0:
  242.7 25.4 reduce-scatter.7
  270.7 22.0 reduce-scatter.5
  296.2 65.0 reduce-scatter.9
Sparse Core Ops, SparseCore 1:
  292.3 132.6 all-reduce.1
where the time goes:
time: 435 us; the launch traced here: 434 us
  blocking collectives  170 us (39%)
  waiting for transfers between devices  101 us (23%)
  matrix products  61.1 us (14%)
  local copies, waits for them, and re-layouts  48.6 us (11%)
  other arithmetic  37.7 us (9%)
  between operations  15.3 us (4%)
    all_gather x3, blocking collectives, joined(): pieces = jax.tree.map(lambda part: lax.all_gather(part, axis), value)  96.3 us
    psum x1, waiting for transfers between devices, on_device(): d_wbias = lax.psum(weight_term, ('row', 'col'))  61.9 us
    unnamed x5, waiting for transfers between devices  38.6 us
    all_gather x1, blocking collectives, on_device(): lax.all_gather(d_out, 'col', axis=1, tiled=True)  32.2 us
    all_gather x1, blocking collectives, on_device(): lax.all_gather(queries, 'col', axis=1, tiled=True)  29.7 us
    convert_element_type x2, other arithmetic, on_device(): (weights * (grad_prob - row_delta[..., None])).astype(jnp.bfloat16)  21 us
    convert_element_type x2, local copies, waits for them, and re-layouts, on_device(): (weights * (grad_prob - row_delta[..., None])).astype(jnp.bfloat16)  14.4 us
    dot_general x1, local copies, waits for them, and re-layouts, on_device(): jnp.dot(flat_pair, w_bias, preferred_element_type=jnp.float32)  12.1 us
  transfers between devices with their start and end apart: 4, of which 2 were waited for; matrix products, arithmetic and copies ran while one was open for 18% of the time, Pallas kernels for 0%

commit v1 on v0

--- a/solution.py
+++ b/solution.py
@@ -7,6 +7,16 @@
 H = 96
 P_SIZE = 512
 HD = 16
+
+
+def gather_around(x, axis, dim):
+    ways, here, step = (lax.axis_size(axis), lax.axis_index(axis), x.shape[dim])
+    dims = [n * ways if d == dim else n for d, n in enumerate(x.shape)]
+    full = lax.dynamic_update_slice_in_dim(jnp.zeros(dims, x.dtype), x, here * step, axis=dim)
+    for far in range(1, ways):
+        x = lax.ppermute(x, axis, [(d, (d + 1) % ways) for d in range(ways)])
+        full = lax.dynamic_update_slice_in_dim(full, x, (here - far) % ways * step, axis=dim)
+    return full
 
 
 def joined(value, axis, join):
@@ -33,7 +43,7 @@
     col_count = pair.shape[1]
     query_full, out_full = (
         lax.all_gather(queries, "col", axis=1, tiled=True),
-        lax.all_gather(d_out, "col", axis=1, tiled=True),
+        gather_around(d_out, "col", 1),
     )
     key_full, value_full = (
         lax.all_gather(keys, "row", axis=1, tiled=True),

time: 435 us -> 470 us (1.080)
  waiting for transfers between devices: 101 us -> 151 us
  blocking collectives: 170 us -> 143 us
  matrix products: 61.1 us -> 66.2 us
    ppermute x0 -> x7, waiting for transfers between devices: none -> 40.3 us  [gather_around(): x = lax.ppermute(x, axis, [(d, (d + 1) % ways) for d in range(ways)])]
    all_gather x1 -> x0, blocking collectives: 32.2 us -> none  [on_device(): lax.all_gather(d_out, 'col', axis=1, tiled=True)]
    psum x1, waiting for transfers between devices: 61.9 us -> 76.3 us  [on_device(): d_wbias = lax.psum(weight_term, ('row', 'col'))]
    all_gather x3, blocking collectives: 96.3 us -> 102 us  [joined(): pieces = jax.tree.map(lambda part: lax.all_gather(part, axis), value)]
  transfers between devices with their start and end apart: 4 -> 11, of which waited for: 2 -> 8; matrix products, arithmetic and copies ran while one was open for 18% -> 25% of each run, Pallas kernels for 0% -> 0%
where the time goes in v1:
time: 470 us; the launch traced here: 469 us
  waiting for transfers between devices  151 us (32%)
  blocking collectives  143 us (30%)
  matrix products  66.2 us (14%)
  local copies, waits for them, and re-layouts  52.6 us (11%)
  other arithmetic  37.7 us (8%)
  between operations  15.7 us (3%)
    all_gather x3, blocking collectives, joined(): pieces = jax.tree.map(lambda part: lax.all_gather(part, axis), value)  102 us
    psum x1, waiting for transfers between devices, on_device(): d_wbias = lax.psum(weight_term, ('row', 'col'))  76.3 us
    ppermute x7, waiting for transfers between devices, gather_around(): x = lax.ppermute(x, axis, [(d, (d + 1) % ways) for d in range(ways)])  40.3 us
    unnamed x5, waiting for transfers between devices  34.6 us
    all_gather x1, blocking collectives, on_device(): lax.all_gather(queries, 'col', axis=1, tiled=True)  29.7 us
    convert_element_type x2, other arithmetic, on_device(): (weights * (grad_prob - row_delta[..., None])).astype(jnp.bfloat16)  20.9 us
    convert_element_type x2, local copies, waits for them, and re-layouts, on_device(): (weights * (grad_prob - row_delta[..., None])).astype(jnp.bfloat16)  14.5 us
    dot_general x1, matrix products, on_device(): jnp.einsum('ihd,jhd->hij', query_heads, key_heads, preferred_element_type...  12.3 us
  transfers between devices with their start and end apart: 11, of which 8 were waited for; matrix products, arithmetic and copies ran while one was open for 25% of the time, Pallas kernels for 0%

profile of v1, /device:TPU:8, one launch (start us, length us, event | category | flops | bytes accessed | tf_op | source)
XLA Modules:
  0.0 468.6 jit_solution(5849390353040049422)
XLA Ops:
  10.8 11.2 %fusion.11 = f32[192,96,96]{2,1,0:T(8,128)} fusion(bf16[192,96,512]{2,1,0:T(8,128)(2,1)} %param.8, bf16[512,96]{0,1:T(8,128)(2,1)S(1)} %copy-done), kind=kOutput, calls=%fused_computation.27 | convolution fusion | flops 1811939328 | bytes 26050560 | tf_op jit(solution)/shard_map/dot_general | solution.py:57
  22.0 12.1 %copy.54 = f32[192,96,96]{0,1,2:T(8,128)} copy(f32[192,96,96]{2,1,0:T(8,128)} %fusion.11) | data formatting | bytes 14155776 | tf_op jit(solution)/shard_map/dot_general | solution.py:57
  34.2 29.7 %all_gather.27 = bf16[192,1536]{0,1:T(8,128)(2,1)S(1)} all-gather(bf16[192,192]{0,1:T(8,128)(2,1)S(1)} %copy.52), channel_id=1, replica_groups=mesh['row'=4,'col'=8] {'col'}, dimensions={1}, use_global_device_ids=true | all-gather | bytes 663552 | tf_op jit(solution)/shard_map/all_gather | solution.py:45
  70.1 12.3 %fusion.13 = (f32[96,192]{1,0:T(8,128)S(1)}, f32[96,192,96]{1,2,0:T(8,128)}, f32[96,192,96]{1,2,0:T(8,128)}) fusion(f32[192,96,96]{0,1,2:T(8,128)} %copy.54, bf16[192,96,16]{0,2,1:T(8,128)(2,1)S(1)} %bitcast.92, bf16[96,96,16]{0,2,1:T(8,128)(2,1)S(1)} %bitcast.96), kind=kOutput, calls=%fused_computation.37 | convolution fusion | flops 61913088 | bytes 22192128 | tf_op jit(solution)/shard_map/ihd,jhd->hij/dot_general | solution.py:61
  82.4 32.3 %all-gather = f32[768,192]{1,0:T(8,128)S(1)} all-gather(f32[96,192]{1,0:T(8,128)S(1)} %get-tuple-element.65), channel_id=2, replica_groups=mesh['row'=4,'col'=8] {'col'}, dimensions={0}, use_global_device_ids=true | all-gather | bytes 663552 | tf_op jit(solution)/shard_map/all_gather | solution.py:23
  122.0 6.1 %collective-permute-done.1 = bf16[192,192]{1,0:T(8,128)(2,1)S(1)} collective-permute-done((bf16[192,192]{1,0:T(8,128)(2,1)}, bf16[192,192]{1,0:T(8,128)(2,1)S(1)}, u32[]{:S(2)}, u32[]{:S(2)}) %collective-permute-start.1) | collective-permute-done | bytes 73760 | tf_op jit(solution)/shard_map/ppermute | solution.py:17
  135.0 6.4 %collective-permute-done.3 = bf16[192,192]{1,0:T(8,128)(2,1)S(1)} collective-permute-done((bf16[192,192]{1,0:T(8,128)(2,1)}, bf16[192,192]{1,0:T(8,128)(2,1)S(1)}, u32[]{:S(2)}, u32[]{:S(2)}) %collective-permute-start.3) | collective-permute-done | bytes 73760 | tf_op jit(solution)/shard_map/ppermute | solution.py:17
  141.6 7.4 %collective-permute-done.4 = bf16[192,192]{1,0:T(8,128)(2,1)} collective-permute-done((bf16[192,192]{1,0:T(8,128)(2,1)S(1)}, bf16[192,192]{1,0:T(8,128)(2,1)}, u32[]{:S(2)}, u32[]{:S(2)}) %collective-permute-start.4) | collective-permute-done | bytes 73760 | tf_op jit(solution)/shard_map/ppermute | solution.py:17
  150.0 7.5 %collective-permute-done.5 = bf16[192,192]{1,0:T(8,128)(2,1)S(1)} collective-permute-done((bf16[192,192]{1,0:T(8,128)(2,1)}, bf16[192,192]{1,0:T(8,128)(2,1)S(1)}, u32[]{:S(2)}, u32[]{:S(2)}) %collective-permute-start.5) | collective-permute-done | bytes 73760 | tf_op jit(solution)/shard_map/ppermute | solution.py:17
  157.7 7.4 %collective-permute-done.6 = bf16[192,192]{1,0:T(8,128)(2,1)} collective-permute-done((bf16[192,192]{1,0:T(8,128)(2,1)S(1)}, bf16[192,192]{1,0:T(8,128)(2,1)}, u32[]{:S(2)}, u32[]{:S(2)}) %collective-permute-start.6) | collective-permute-done | bytes 73760 | tf_op jit(solution)/shard_map/ppermute | solution.py:17
  166.1 7.6 %multiply_reduce_fusion = (f32[96,192]{1,0:T(8,128)S(1)}, f32[96,192]{1,0:T(8,128)S(1)}, f32[96,192,96]{1,2,0:T(8,128)}) fusion(f32[96,192,96]{1,2,0:T(8,128)} %get-tuple-element.66, f32[96,192]{1,0:T(8,128)S(1)} %get-tuple-element.65, bf16[192,96,16]{0,2,1:T(8,128)(2,1)S(1)} %bitcast.98, bf16[96,96,16]{0,2,1:T(8,128)(2,1)S(1)} %bitcast.103), kind=kOutput, calls=%fused_computation.19 | convolution fusion | flops 63664128 | bytes 15261696 | tf_op jit(solution)/shard_map/ihd,jhd->hij/dot_general | solution.py:64
  173.7 37.3 %all-gather.1 = f32[768,192]{1,0:T(8,128)S(1)} all-gather(f32[96,192]{1,0:T(8,128)S(1)} %get-tuple-element.48), channel_id=3, replica_groups=mesh['row'=4,'col'=8] {'col'}, dimensions={0}, use_global_device_ids=true | all-gather | bytes 663552 | tf_op jit(solution)/shard_map/all_gather | solution.py:23
  211.9 31.9 %all-gather.2 = f32[768,192]{1,0:T(8,128)S(1)} all-gather(f32[96,192]{1,0:T(8,128)S(1)} %get-tuple-element.47), channel_id=4, replica_groups=mesh['row'=4,'col'=8] {'col'}, dimensions={0}, use_global_device_ids=true | all-gather | bytes 663552 | tf_op jit(solution)/shard_map/all_gather | solution.py:23
  244.8 13.8 %while.14 = (s32[]{:T(128)}, f32[96,192]{1,0:T(8,128)S(1)}, f32[96,192]{1,0:T(8,128)S(1)}, f32[96,192]{1,0:T(8,128)S(1)}, f32[7,96,192]{2,1,0:T(8,128)S(1)}, /*i...) while((s32[]{:T(128)}, f32[96,192]{1,0:T(8,128)S(1)}, f32[96,192]{1,0:T(8,128)S(1)}, ...), condition=%wide.region_4.5_spmd, body=%wide.region_3.4_spmd.sunk | while | flops 202754 | bytes 1032285 | solution.py:26
  258.6 6.1 %fusion.9 = f32[96,16,96]{2,1,0:T(8,128)} fusion(bf16[192,96,16]{0,2,1:T(8,128)(2,1)S(1)} %bitcast.99, f32[96,192,96]{1,2,0:T(8,128)} %get-tuple-element.66, f32[96,192]{1,0:T(8,128)S(1)} %get-tuple-element.45, f32[96,192]{1,0:T(8,128)S(1)} %get-tuple-element.44), kind=kOutput, calls=%fused_computation.22 | convolution fusion | flops 61931520 | bytes 8404992 | tf_op jit(solution)/shard_map/hij,ihd->jhd/dot_general | solution.py:95
  267.1 8.0 %multiply_convert_fusion = bf16[96,192,96]{1,2,0:T(8,128)(2,1)S(1)} fusion(f32[96,192,96]{1,2,0:T(8,128)} %get-tuple-element.68, f32[96,192]{1,0:T(8,128)S(1)} %div.21, f32[96,192]{1,0:T(8,128)S(1)} %get-tuple-element.45, f32[96,192,96]{1,2,0:T(8,128)} %get-tuple-element.66, f32[96,192]{1,0:T(8,128)S(1)} %get-tuple-element.44), kind=kLoop, calls=%fused_computation.17 | loop fusion | flops 8847360 | bytes 17915904 | tf_op jit(solution)/shard_map/convert_element_type | solution.py:77
  284.1 12.9 %fusion.4 = bf16[192,96,96]{0,1,2:T(8,128)(2,1)} fusion(f32[96,192,96]{1,2,0:T(8,128)} %get-tuple-element.68, f32[192,96,96]{0,1,2:T(8,128)} %copy.54, f32[96,192,96]{1,2,0:T(8,128)} %get-tuple-element.67, f32[192,96]{0,1:T(8,128)S(1)} %bitcast.104, f32[192,96]{0,1:T(8,128)S(1)} %bitcast.91, f32[192,96]{0,1:T(8,128)S(1)} %bitcast.90), kind=kLoop, calls=%fused_computation.11 | loop fusion | flops 12386304 | bytes 24993792 | tf_op jit(solution)/shard_map/convert_element_type | solution.py:77
  297.1 6.8 %copy.65 = bf16[192,96,96]{1,0,2:T(8,128)(2,1)} copy(bf16[192,96,96]{0,1,2:T(8,128)(2,1)} %fusion.4) | data formatting | bytes 7077888 | tf_op jit(solution)/shard_map/convert_element_type | solution.py:77
  303.9 7.7 %copy.66 = bf16[192,96,96]{1,2,0:T(8,128)(2,1)} copy(bf16[192,96,96]{0,1,2:T(8,128)(2,1)} %fusion.4) | data formatting | bytes 7077888 | tf_op jit(solution)/shard_map/convert_element_type | solution.py:77
  311.6 9.2 %reshape.49 = bf16[18432,96]{0,1:T(8,128)(2,1)} reshape(bf16[192,96,96]{1,0,2:T(8,128)(2,1)} %copy.65) | data formatting | bytes 7077888 | tf_op jit(solution)/shard_map/reshape | solution.py:79
  320.8 11.8 %convolution_bitcast_fusion = f32[512,96]{0,1:T(8,128)} fusion(bf16[192,96,96]{1,2,0:T(8,128)(2,1)} %copy.66, bf16[192,96,512]{2,1,0:T(8,128)(2,1)} %param.8), kind=kOutput, calls=%fused_computation.26 | convolution fusion | flops 1811939328 | bytes 22609920 | tf_op jit(solution)/shard_map/dot_general | solution.py:85
  332.6 11.6 %convolution_convert_fusion = bf16[18432,512]{1,0:T(8,128)(2,1)} fusion(bf16[18432,96]{0,1:T(8,128)(2,1)} %reshape.49, bf16[512,96]{0,1:T(8,128)(2,1)S(1)} %copy-done), kind=kOutput, calls=%fused_computation.8 | convolution fusion | flops 1821376512 | bytes 22511616 | tf_op jit(solution)/shard_map/dot_general | solution.py:81
  347.3 34.5 %reduce-scatter.10.cloned.1.call-done = f32[192,192]{1,0:T(8,128)} async-done(((f32[1536,192]{1,0:T(8,128)}), f32[192,192]{1,0:T(8,128)}) %reduce-scatter.10.cloned.1.call-update) | async-done | bytes 147472
  383.5 76.3 %all-reduce.2.cloned.1.call-done = f32[512,96]{0,1:T(8,128)} async-done(((f32[512,96]{0,1:T(8,128)}), f32[512,96]{0,1:T(8,128)}) %all-reduce.2.cloned.1.call-update) | async-done | bytes 196624 | tf_op jit(solution)/shard_map/psum | solution.py:86
  (87 shorter events, 58.7 us)
Async XLA Ops:
  8.0 2.8 copy-start
  8.0 336.2 %reduce-scatter.8.cloned.1.call-start = ((), (), s32[]{:S(2)}) async-start(), calls=%async_computation.5 | async-start | bytes 737280 | tf_op jit(solution)/shard_map/reduce_scatter | solution.py:101
  8.1 112.9 %collective-permute-start = (bf16[192,192]{1,0:T(8,128)(2,1)}, bf16[192,192]{1,0:T(8,128)(2,1)}, u32[]{:S(2)}, u32[]{:S(2)}) collective-permute-start(bf16[192,192]{1,0:T(8,128)(2,1)} %param.13), channel_id=1, source_target_pairs={{0,1},{1,2},{2,3},{3,4},{4,5},{5,6},{6,7},{7,0},{8,9},{9,10},{10,1... | collective-permute-start | bytes 221192 | tf_op jit(solution)/shard_map/ppermute | solution.py:17
  22.0 12.1 %copy-start.2 = (bf16[192,192]{1,0:T(8,128)(2,1)S(1)}, bf16[192,192]{1,0:T(8,128)(2,1)}, u32[]{:S(2)}) copy-start(bf16[192,192]{1,0:T(8,128)(2,1)} %param.10) | copy-start | bytes 221188
  22.0 41.9 %copy-start.3 = (bf16[96,384]{1,0:T(8,128)(2,1)S(1)}, bf16[96,384]{1,0:T(8,128)(2,1)}, u32[]{:S(2)}) copy-start(bf16[96,384]{1,0:T(8,128)(2,1)} %param.11) | copy-start | bytes 221188
  70.1 44.6 %copy-start.4 = (bf16[96,384]{1,0:T(8,128)(2,1)S(1)}, bf16[96,384]{1,0:T(8,128)(2,1)}, u32[]{:S(2)}) copy-start(bf16[96,384]{1,0:T(8,128)(2,1)} %param.12) | copy-start | bytes 221188
  121.9 6.2 %collective-permute-start.1 = (bf16[192,192]{1,0:T(8,128)(2,1)}, bf16[192,192]{1,0:T(8,128)(2,1)S(1)}, u32[]{:S(2)}, u32[]{:S(2)}) collective-permute-start(bf16[192,192]{1,0:T(8,128)(2,1)} %collective-permute-done), channel_id=1, source_target_pairs={{0,1},{1,2},{2,3},{3,4},{4,5},{5,6},{6,7},{7,0},{8,9},{9,10},{10,1... | collective-permute-start | bytes 221192 | tf_op jit(solution)/shard_map/ppermute | solution.py:17
  128.3 5.7 %collective-permute-start.2 = (bf16[192,192]{1,0:T(8,128)(2,1)S(1)}, bf16[192,192]{1,0:T(8,128)(2,1)}, u32[]{:S(2)}, u32[]{:S(2)}) collective-permute-start(bf16[192,192]{1,0:T(8,128)(2,1)S(1)} %collective-permute-done.1), channel_id=1, source_target_pairs={{0,1},{1,2},{2,3},{3,4},{4,5},{5,6},{6,7},{7,0},{8,9},{9,10},{10,1... | collective-permute-start | bytes 221192 | tf_op jit(solution)/shard_map/ppermute | solution.py:17
  134.9 6.5 %collective-permute-start.3 = (bf16[192,192]{1,0:T(8,128)(2,1)}, bf16[192,192]{1,0:T(8,128)(2,1)S(1)}, u32[]{:S(2)}, u32[]{:S(2)}) collective-permute-start(bf16[192,192]{1,0:T(8,128)(2,1)} %collective-permute-done.2), channel_id=1, source_target_pairs={{0,1},{1,2},{2,3},{3,4},{4,5},{5,6},{6,7},{7,0},{8,9},{9,10},{10,1... | collective-permute-start | bytes 221192 | tf_op jit(solution)/shard_map/ppermute | solution.py:17
  141.5 7.5 %collective-permute-start.4 = (bf16[192,192]{1,0:T(8,128)(2,1)S(1)}, bf16[192,192]{1,0:T(8,128)(2,1)}, u32[]{:S(2)}, u32[]{:S(2)}) collective-permute-start(bf16[192,192]{1,0:T(8,128)(2,1)S(1)} %collective-permute-done.3), channel_id=1, source_target_pairs={{0,1},{1,2},{2,3},{3,4},{4,5},{5,6},{6,7},{7,0},{8,9},{9,10},{10,1... | collective-permute-start | bytes 221192 | tf_op jit(solution)/shard_map/ppermute | solution.py:17
  150.0 7.6 %collective-permute-start.5 = (bf16[192,192]{1,0:T(8,128)(2,1)}, bf16[192,192]{1,0:T(8,128)(2,1)S(1)}, u32[]{:S(2)}, u32[]{:S(2)}) collective-permute-start(bf16[192,192]{1,0:T(8,128)(2,1)} %collective-permute-done.4), channel_id=1, source_target_pairs={{0,1},{1,2},{2,3},{3,4},{4,5},{5,6},{6,7},{7,0},{8,9},{9,10},{10,1... | collective-permute-start | bytes 221192 | tf_op jit(solution)/shard_map/ppermute | solution.py:17
  157.6 7.5 %collective-permute-start.6 = (bf16[192,192]{1,0:T(8,128)(2,1)S(1)}, bf16[192,192]{1,0:T(8,128)(2,1)}, u32[]{:S(2)}, u32[]{:S(2)}) collective-permute-start(bf16[192,192]{1,0:T(8,128)(2,1)S(1)} %collective-permute-done.5), channel_id=1, source_target_pairs={{0,1},{1,2},{2,3},{3,4},{4,5},{5,6},{6,7},{7,0},{8,9},{9,10},{10,1... | collective-permute-start | bytes 221192 | tf_op jit(solution)/shard_map/ppermute | solution.py:17
  267.0 78.8 %reduce-scatter.6.cloned.1.call-start = ((), (), s32[]{:S(2)}) async-start(), calls=%async_computation.4 | async-start | bytes 737280 | tf_op jit(solution)/shard_map/reduce_scatter | solution.py:100
  275.1 2.2 copy-start.1
  279.7 102.1 %reduce-scatter.10.cloned.1.call-start = ((), (), s32[]{:S(2)}) async-start(), calls=%async_computation.6 | async-start | bytes 1769472
  284.1 175.7 %all-reduce.2.cloned.1.call-start = ((), (), s32[]{:S(2)}) async-start(), calls=%async_computation.3 | async-start | bytes 393216 | tf_op jit(solution)/shard_map/psum | solution.py:86
Sparse Core Ops, SparseCore 0:
  267.1 21.4 reduce-scatter.7
  291.1 22.0 reduce-scatter.5
  316.6 65.1 reduce-scatter.9
Sparse Core Ops, SparseCore 1:
  332.7 127.0 all-reduce.1
